TPU v7x, 256 devices: a whole 4x4x8 slice. The times are simulated.
256 devices in a mesh: chan: 4 (over x_hi, core), tm: 16 (over x_lo, z), stat: 4 (over y).
Axes of the slice: x: 4 (x_hi: 2, x_lo: 2; x = x_hi * 2 + x_lo), y: 4, z: 8, core: 2. Of those that a mesh axis runs over, the one named last changes fastest.
Arguments:
- voltages: bfloat16 [8, 2, 512, 32768], P('chan', None, 'stat', 'tm'), may hold values from -6 to 6
- ref_index: int32 [8], replicated, may hold values from 0 to 511
- positions: int32 [32768], P('tm'), may hold values from 0 to 255
- aperture_weight: float32 [256], replicated, may hold values from 0.25 to 4
Outputs:
- coefficients: float32 [512, 8, 8, 128], P(('stat', 'tm', 'chan'))
Inputs may be any that keep to these rules, and one draw needn't show every extreme that they name: Each entry of ref_index is a station number; entries may repeat. Each entry of positions is a raster cell index of the 16 x 16 raster.
All inputs are finite; a program needn't handle non-finite values.
Results may differ from a plain program's by a relative error of at most 0.0003.
Values may be sent and summed in bfloat16 or wider, within the bound.
A program may use at most 128 MiB of HBM per device.

v0:
```python
import functools
import math

import jax
import jax.numpy as jnp
import numpy as np
from jax import lax
from jax.experimental import pallas as pl
from jax.experimental.pallas import tpu as pltpu
from jax.sharding import PartitionSpec as P

RASTER = 16
CELLS = RASTER * RASTER
ZERN = 64
REFS = 8
MESH = pl.DeviceIdType.MESH
F32 = jnp.float32
BF16 = jnp.bfloat16
HIGHEST = lax.Precision.HIGHEST
NT = (((1,), (1,)), ((), ()))


def zernike_table():
    cells = np.arange(CELLS)
    x = (cells // RASTER - RASTER // 2 + 0.5) / (RASTER / 2.0)
    y = (cells % RASTER - RASTER // 2 + 0.5) / (RASTER / 2.0)
    radius_sq = x * x + y * y
    rows = []
    degree = 0
    while len(rows) < ZERN:
        for azimuth in range(-degree, degree + 1, 2):
            if len(rows) == ZERN:
                break
            order = abs(azimuth)
            power = (x + 1j * y) ** order
            radial = np.zeros_like(x)
            for k in range((degree - order) // 2 + 1):
                weight = (-1) ** k * math.factorial(degree - k)
                weight /= math.factorial(k)
                weight /= math.factorial((degree + order) // 2 - k)
                weight /= math.factorial((degree - order) // 2 - k)
                radial = radial + weight * radius_sq ** ((degree - 2 * k - order) // 2)
            if azimuth > 0:
                row = radial * power.real * math.sqrt(2.0 * (degree + 1))
            elif azimuth < 0:
                row = radial * power.imag * math.sqrt(2.0 * (degree + 1))
            else:
                row = radial * math.sqrt(degree + 1.0)
            rows.append(np.where(radius_sq <= 1.0, row, 0.0))
        degree += 1
    return np.stack(rows).astype(np.float32)


def dft_table(scale):
    cells = np.arange(CELLS)
    a = cells // RASTER - RASTER // 2
    b = cells % RASTER - RASTER // 2
    phases = (a[:, None] * a[None, :] + b[:, None] * b[None, :]) % RASTER
    angles = phases * (2.0 * math.pi / RASTER)
    both = np.concatenate([np.cos(angles), -np.sin(angles)], axis=1)
    return (both * scale).astype(np.float32)


def fit_operator(zern, weight, dft):
    weighted = zern * weight
    gram = lax.dot_general(weighted, zern, NT, precision=HIGHEST, preferred_element_type=F32)
    rows = lax.broadcasted_iota(jnp.int32, (ZERN, ZERN), 0)
    cols = lax.broadcasted_iota(jnp.int32, (ZERN, ZERN), 1)
    both = jnp.concatenate([gram, (rows == cols).astype(F32)], axis=1)
    row_ids = lax.broadcasted_iota(jnp.int32, (ZERN, 2 * ZERN), 0)
    for k in range(ZERN):
        pivot_row = both[k : k + 1, :] * (1.0 / both[k : k + 1, k : k + 1])
        reduced = both - both[:, k : k + 1] * pivot_row
        both = jnp.where(row_ids == k, pivot_row, reduced)
    padded = jnp.concatenate([jnp.zeros_like(weighted), weighted], axis=0)
    solve = jnp.dot(both, padded, precision=HIGHEST, preferred_element_type=F32)
    return jnp.dot(solve, dft, precision=HIGHEST, preferred_element_type=F32)


def exchange_kernel(
    volt_ref, index_ref, zern_ref, weight_ref, dft_ref, out_ref, table_ref,
    own, got, send_sem, recv_sem,
):
    n = lax.axis_size("stat")
    me = lax.axis_index("stat")
    chans, parts, stations, times = volt_ref.shape
    barrier = pltpu.get_barrier_semaphore()
    for d in range(1, n):
        pl.semaphore_signal(
            barrier, inc=1, device_id={"stat": lax.rem(me + d, n)}, device_id_type=MESH
        )
    cols = lax.broadcasted_iota(jnp.int32, (2 * REFS, parts * stations), 1)
    rows = lax.broadcasted_iota(jnp.int32, (2 * REFS, parts * stations), 0)
    wanted = index_ref[...] - me * stations
    inside = (wanted >= 0) & (wanted < stations)
    target = jnp.where(inside, wanted, -parts * stations) + (rows // REFS) * stations
    select = jnp.where(cols == target, 1.0, 0.0).astype(BF16)
    for c in range(chans):
        block = volt_ref[c].reshape(parts * stations, times)
        own[c] = jnp.dot(select, block, preferred_element_type=F32).astype(BF16)
    pl.semaphore_wait(barrier, n - 1)
    copies = []
    for d in range(1, n):
        copy = pltpu.make_async_remote_copy(
            src_ref=own, dst_ref=got.at[d - 1], send_sem=send_sem.at[d - 1],
            recv_sem=recv_sem.at[d - 1], device_id={"stat": lax.rem(me + d, n)},
            device_id_type=MESH,
        )
        copy.start()
        copies.append(copy)
    operator = fit_operator(zern_ref[...], weight_ref[...], dft_ref[...])
    table = jnp.concatenate([operator[:, :CELLS], operator[:, CELLS:]], axis=0)
    high = table.astype(BF16)
    table_ref[: 2 * ZERN, :] = high
    table_ref[2 * ZERN :, :] = (table - high.astype(F32)).astype(BF16)
    for copy in copies:
        copy.wait()
    for c in range(chans):
        total = own[c].astype(F32)
        for d in range(1, n):
            total = total + got[d - 1, c].astype(F32)
        out_ref[c] = total


def correlate_kernel(volt_ref, refs_ref, pos_ref, table_ref, part_ref, field, left_a, left_b):
    chans, parts, stations, times = volt_ref.shape
    step = 512
    for t in range(0, times, step):
        cells = lax.broadcasted_iota(jnp.int32, (CELLS, step), 0)
        onehot = jnp.where(cells == pos_ref[:, t : t + step], 1.0, 0.0).astype(BF16)
        both = jnp.dot(table_ref[...], onehot, preferred_element_type=F32)
        field[:, t : t + step] = both[: 2 * ZERN] + both[2 * ZERN :]
    lane = lax.broadcasted_iota(jnp.int32, (stations, 2 * ZERN), 1)
    rows, width = 16, 256

    def build(left, c, r):
        for t in range(0, times, width):
            at = slice(t, t + width)
            re = jnp.broadcast_to(refs_ref[c, pl.ds(r, 1), at], (rows, width))
            im = jnp.broadcast_to(refs_ref[c, pl.ds(r + REFS, 1), at], (rows, width))
            for j in range(0, ZERN, rows):
                h = field[j : j + rows, at]
                g = field[ZERN + j : ZERN + j + rows, at]
                for base, value in ((j, re * h + im * g), (ZERN + j, re * g - im * h)):
                    high = value.astype(BF16)
                    left[base : base + rows, at] = high
                    low = (value - high.astype(F32)).astype(BF16)
                    left[2 * ZERN + base : 2 * ZERN + base + rows, at] = low

    def multiply(left, c, r):
        block = volt_ref[c].reshape(parts * stations, times)
        both = lax.dot_general(block, left[...], NT, preferred_element_type=F32)
        both = both[:, : 2 * ZERN] + both[:, 2 * ZERN :]
        real, imag = both[:stations], pltpu.roll(both[stations:], ZERN, 1)
        out = real + jnp.where(lane < ZERN, -imag, imag)
        part_ref[pl.ds(c * REFS + r, stations, stride=chans * REFS), :] = out

    build(left_a, 0, 0)
    for c in range(chans):

        def body(i, carry, c=c):
            r = 2 * i
            build(left_b, c, r + 1)
            multiply(left_a, c, r)
            follow = r + 2
            wrap = follow == REFS
            build(left_a, jnp.where(wrap, min(c + 1, chans - 1), c), jnp.where(wrap, 0, follow))
            multiply(left_b, c, r + 1)
            return carry

        lax.fori_loop(0, REFS // 2, body, 0)


def regroup_kernel(part_ref, out_ref, side, held, got, side_send, side_recv, send_sem, recv_sem):
    tm, q = lax.axis_index("tm"), lax.axis_index("chan")
    n_tm, n_q = lax.axis_size("tm"), lax.axis_size("chan")
    n_z = n_tm // 2
    x, z = tm // n_z, lax.rem(tm, n_z)
    other = 1 - x
    chunk = part_ref.shape[0] // (n_tm * n_q)
    group = chunk * n_q
    half = group * n_z
    barrier = pltpu.get_barrier_semaphore()
    partner = {"tm": other * n_z + z}
    pl.semaphore_signal(barrier, inc=1, device_id=partner, device_id_type=MESH)

    def peer(dz, dq):
        return {"tm": x * n_z + lax.rem(z + dz, n_z), "chan": lax.rem(q + dq, n_q)}

    order = sorted(range(n_z), key=lambda d: -min(d, n_z - d))
    pairs = [(dz, dq) for dz in order for dq in range(n_q) if dz or dq]
    for dz, dq in pairs:
        pl.semaphore_signal(barrier, inc=1, device_id=peer(dz, dq), device_id_type=MESH)
    pl.semaphore_wait(barrier, len(pairs) + 1)

    across = []
    for k, dz in enumerate(order):
        to = lax.rem(z + dz, n_z)
        copy = pltpu.make_async_remote_copy(
            src_ref=part_ref.at[pl.ds(pl.multiple_of(other * half + to * group, group), group)],
            dst_ref=side.at[k], send_sem=side_send.at[k], recv_sem=side_recv.at[k],
            device_id=partner, device_id_type=MESH,
        )
        copy.start()
        across.append(copy)
    copies = []
    for k, dz in enumerate(order):
        across[k].wait_recv()
        to = lax.rem(z + dz, n_z)
        mine = part_ref[pl.ds(pl.multiple_of(x * half + to * group, group), group)]
        held[k] = mine + side[k]
        for dq in range(n_q):
            if not (dz or dq):
                continue
            slot = dz * n_q + dq
            aim = lax.rem(q + dq, n_q)
            copy = pltpu.make_async_remote_copy(
                src_ref=held.at[k, pl.ds(pl.multiple_of(aim * chunk, chunk), chunk)],
                dst_ref=got.at[slot], send_sem=send_sem.at[slot], recv_sem=recv_sem.at[slot],
                device_id=peer(dz, dq), device_id_type=MESH,
            )
            copy.start()
            copies.append(copy)
    for copy in copies:
        copy.wait_recv()
    stations = out_ref.shape[0]
    rows = chunk // stations
    for dq in range(n_q):
        total = None
        for dz in range(n_z):
            if dz or dq:
                term = got[dz * n_q + dq]
            else:
                term = held[n_z - 1, pl.ds(pl.multiple_of(q * chunk, chunk), chunk)]
            total = term if total is None else total + term
        origin = lax.rem(q - dq + n_q, n_q)
        for s in range(stations):
            out_ref[s, pl.ds(pl.multiple_of(origin * rows, rows), rows)] = total[
                s * rows : (s + 1) * rows
            ]
    for copy in across + copies:
        copy.wait_send()


def on_device(voltages, ref_index, positions, aperture_weight):
    chans, parts, stations, times = voltages.shape
    n_stat, n_tm, n_q = lax.axis_size("stat"), lax.axis_size("tm"), lax.axis_size("chan")
    scale = (n_tm * times / CELLS) ** (-0.5)
    zern = jnp.asarray(zernike_table())
    dft = jnp.asarray(dft_table(scale))
    index = jnp.tile(ref_index, 2)[:, None]
    vmem = pl.BlockSpec(memory_space=pltpu.VMEM)
    dma = pltpu.SemaphoreType.DMA
    refs, table = pl.pallas_call(
        exchange_kernel,
        out_shape=(
            jax.ShapeDtypeStruct((chans, 2 * REFS, times), F32),
            jax.ShapeDtypeStruct((4 * ZERN, CELLS), BF16),
        ),
        in_specs=[vmem] * 5,
        out_specs=(vmem, vmem),
        scratch_shapes=[
            pltpu.VMEM((chans, 2 * REFS, times), BF16),
            pltpu.VMEM((n_stat - 1, chans, 2 * REFS, times), BF16),
            dma((n_stat - 1,)),
            dma((n_stat - 1,)),
        ],
        compiler_params=pltpu.CompilerParams(collective_id=0, has_side_effects=True),
        name="exchange",
    )(voltages, index, zern, aperture_weight[None, :], dft)
    part = pl.pallas_call(
        correlate_kernel,
        out_shape=jax.ShapeDtypeStruct((stations * chans * REFS, 2 * ZERN), F32),
        in_specs=[vmem] * 4,
        out_specs=vmem,
        scratch_shapes=[
            pltpu.VMEM((2 * ZERN, times), F32),
            pltpu.VMEM((4 * ZERN, times), BF16),
            pltpu.VMEM((4 * ZERN, times), BF16),
        ],
        name="correlate",
    )(voltages, refs, positions[None, :], table)
    n_z = n_tm // 2
    rows = stations * chans * REFS
    chunk = rows // (n_tm * n_q)
    own = stations // (n_tm * n_q)
    out = pl.pallas_call(
        regroup_kernel,
        out_shape=jax.ShapeDtypeStruct((own, n_q * chans * REFS, 2 * ZERN), F32),
        in_specs=[vmem],
        out_specs=vmem,
        scratch_shapes=[
            pltpu.VMEM((n_z, chunk * n_q, 2 * ZERN), F32),
            pltpu.VMEM((n_z, chunk * n_q, 2 * ZERN), F32),
            pltpu.VMEM((n_z * n_q, chunk, 2 * ZERN), F32),
            dma((n_z,)),
            dma((n_z,)),
            dma((n_z * n_q,)),
            dma((n_z * n_q,)),
        ],
        compiler_params=pltpu.CompilerParams(collective_id=1, has_side_effects=True),
        name="regroup",
    )(part)
    return out.reshape(own, n_q * chans, REFS, 2 * ZERN)


def solution(mesh):
    in_specs = (P("chan", None, "stat", "tm"), P(), P("tm"), P())
    out_specs = P(("stat", "tm", "chan"), None, None, None)
    return jax.shard_map(
        on_device, mesh=mesh, in_specs=in_specs, out_specs=out_specs, check_vma=False
    )
```

profile of v0, /device:TPU:1, one launch (start us, length us, event | category | flops | bytes accessed | tf_op | source)
XLA Modules:
  0.0 61.2 jit_solution(14462250809327102572)
XLA Ops:
  0.0 0.7 %tile.2 = s32[2,8]{1,0:T(2,128)S(1)} broadcast(s32[8]{0:T(128)} %param.7), dimensions={1} | broadcast | bytes 96 | tf_op jit(solution)/shard_map/tile | solution.py:251
  0.7 0.7 %broadcast_in_dim_tile.4.index_ref = s32[16,1]{1,0:T(8,128)} reshape(s32[2,8]{1,0:T(2,128)S(1)} %tile.2) | data formatting | bytes 128 | tf_op jit(solution)/shard_map/broadcast_in_dim;tile | solution.py:251
  1.3 12.5 %exchange.1 = (f32[2,16,2048]{2,1,0:T(8,128)}, bf16[256,256]{1,0:T(8,128)(2,1)}) custom-call(bf16[2,2,128,2048]{3,2,1,0:T(8,128)(2,1)} %volt_ref.3, s32[16,1]{1,0:T(8,128)} %broadcast_in_dim_tile.4.index_ref, f32[64,256]{1,0:T(8,128)} %constant.4.clone.zern_ref, f32[1,256]{1,0:T(1,128)} %bitcast.5, f32[256,512]{1,0:T(8,128)} %constant.5.clone.dft_ref), custom_call_target="tpu_custom_call" | custom-call | tf_op jit(solution)/shard_map/exchange/pallas_call | solution.py:254
  13.9 10.1 %correlate.1.part_ref = f32[2048,128]{1,0:T(8,128)} custom-call(bf16[2,2,128,2048]{3,2,1,0:T(8,128)(2,1)} %volt_ref.3, f32[2,16,2048]{2,1,0:T(8,128)} %get-tuple-element.7.refs_ref, s32[1,2048]{1,0:T(1,128)} %bitcast.4, bf16[256,256]{1,0:T(8,128)(2,1)} %get-tuple-element.8.table_ref), custom_call_target="tpu_custom_call" | custom-call | tf_op jit(solution)/shard_map/correlate/pallas_call | solution.py:271
  24.0 35.7 %regroup.1 = f32[2,64,128]{2,1,0:T(8,128)} custom-call(f32[2048,128]{1,0:T(8,128)} %correlate.1.part_ref), custom_call_target="tpu_custom_call" | custom-call | tf_op jit(solution)/shard_map/regroup/pallas_call | solution.py:287
  59.8 1.5 %copy.9 = f32[2,8,8,128]{3,2,1,0:T(8,128)} copy(f32[2,8,8,128]{3,2,1,0:T(8,128)} %bitcast.3) | data formatting | bytes 131072
where the time goes:
time: 61.5 us; the launch traced here: 61.2 us
  Pallas kernels  58.4 us (95%)
  local copies, waits for them, and re-layouts  2.81 us (5%)
    pallas_call x1, Pallas kernels, on_device(): pl.pallas_call(regroup_kernel, out_shape=jax.ShapeDtypeStruct((own, n_q *...  35.7 us
    pallas_call x1, Pallas kernels, on_device(): pl.pallas_call(exchange_kernel, out_shape=(jax.ShapeDtypeStruct((chans, 2...  12.5 us
    pallas_call x1, Pallas kernels, on_device(): pl.pallas_call(correlate_kernel, out_shape=jax.ShapeDtypeStruct((stations...  10.1 us
    unnamed x1, local copies, waits for them, and re-layouts  1.47 us
    another operation x2, local copies, waits for them, and re-layouts, on_device(): index = jnp.tile(ref_index, 2)[:, None]  1.34 us

commit v1 on v0

v1 whole, which is shorter than its diff:
```python
import functools
import math

import jax
import jax.numpy as jnp
import numpy as np
from jax import lax
from jax.experimental import pallas as pl
from jax.experimental.pallas import tpu as pltpu
from jax.sharding import PartitionSpec as P

RASTER = 16
CELLS = RASTER * RASTER
ZERN = 64
REFS = 8
MESH = pl.DeviceIdType.MESH
F32 = jnp.float32
BF16 = jnp.bfloat16
HIGHEST = lax.Precision.HIGHEST
NT = (((1,), (1,)), ((), ()))


def zernike_table():
    cells = np.arange(CELLS)
    x = (cells // RASTER - RASTER // 2 + 0.5) / (RASTER / 2.0)
    y = (cells % RASTER - RASTER // 2 + 0.5) / (RASTER / 2.0)
    radius_sq = x * x + y * y
    rows = []
    degree = 0
    while len(rows) < ZERN:
        for azimuth in range(-degree, degree + 1, 2):
            if len(rows) == ZERN:
                break
            order = abs(azimuth)
            power = (x + 1j * y) ** order
            radial = np.zeros_like(x)
            for k in range((degree - order) // 2 + 1):
                weight = (-1) ** k * math.factorial(degree - k)
                weight /= math.factorial(k)
                weight /= math.factorial((degree + order) // 2 - k)
                weight /= math.factorial((degree - order) // 2 - k)
                radial = radial + weight * radius_sq ** ((degree - 2 * k - order) // 2)
            if azimuth > 0:
                row = radial * power.real * math.sqrt(2.0 * (degree + 1))
            elif azimuth < 0:
                row = radial * power.imag * math.sqrt(2.0 * (degree + 1))
            else:
                row = radial * math.sqrt(degree + 1.0)
            rows.append(np.where(radius_sq <= 1.0, row, 0.0))
        degree += 1
    return np.stack(rows).astype(np.float32)


def dft_table(scale):
    cells = np.arange(CELLS)
    a = cells // RASTER - RASTER // 2
    b = cells % RASTER - RASTER // 2
    phases = (a[:, None] * a[None, :] + b[:, None] * b[None, :]) % RASTER
    angles = phases * (2.0 * math.pi / RASTER)
    both = np.concatenate([np.cos(angles), -np.sin(angles)], axis=1)
    return (both * scale).astype(np.float32)


def fit_operator(zern, weight, dft):
    weighted = zern * weight
    gram = lax.dot_general(weighted, zern, NT, precision=HIGHEST, preferred_element_type=F32)
    rows = lax.broadcasted_iota(jnp.int32, (ZERN, ZERN), 0)
    cols = lax.broadcasted_iota(jnp.int32, (ZERN, ZERN), 1)
    both = jnp.concatenate([gram, (rows == cols).astype(F32)], axis=1)
    row_ids = lax.broadcasted_iota(jnp.int32, (ZERN, 2 * ZERN), 0)
    for k in range(ZERN):
        pivot_row = both[k : k + 1, :] * (1.0 / both[k : k + 1, k : k + 1])
        reduced = both - both[:, k : k + 1] * pivot_row
        both = jnp.where(row_ids == k, pivot_row, reduced)
    padded = jnp.concatenate([jnp.zeros_like(weighted), weighted], axis=0)
    solve = jnp.dot(both, padded, precision=HIGHEST, preferred_element_type=F32)
    return jnp.dot(solve, dft, precision=HIGHEST, preferred_element_type=F32)


def exchange_kernel(
    volt_ref, index_ref, zern_ref, weight_ref, dft_ref, out_ref, table_ref,
    own, got, send_sem, recv_sem,
):
    n = lax.axis_size("stat")
    me = lax.axis_index("stat")
    chans, parts, stations, times = volt_ref.shape
    right, left = lax.rem(me + 1, n), lax.rem(me + n - 1, n)
    barrier = pltpu.get_barrier_semaphore()
    for peer in (right, left):
        pl.semaphore_signal(barrier, inc=1, device_id={"stat": peer}, device_id_type=MESH)
    cols = lax.broadcasted_iota(jnp.int32, (2 * REFS, parts * stations), 1)
    rows = lax.broadcasted_iota(jnp.int32, (2 * REFS, parts * stations), 0)
    wanted = jnp.zeros_like(rows)
    for r in range(REFS):
        wanted = jnp.where(lax.rem(rows, REFS) == r, index_ref[r], wanted)
    wanted = wanted - me * stations
    inside = (wanted >= 0) & (wanted < stations)
    target = jnp.where(inside, wanted, -parts * stations) + (rows // REFS) * stations
    select = jnp.where(cols == target, 1.0, 0.0).astype(BF16)
    for c in range(chans):
        block = volt_ref[c].reshape(parts * stations, times)
        own[c] = jnp.dot(select, block, preferred_element_type=F32).astype(BF16)
    pl.semaphore_wait(barrier, 2)

    def send(src, slot, c, peer):
        copy = pltpu.make_async_remote_copy(
            src_ref=src, dst_ref=got.at[slot, c], send_sem=send_sem.at[slot, c],
            recv_sem=recv_sem.at[slot, c], device_id={"stat": peer}, device_id_type=MESH,
        )
        copy.start()
        return copy

    copies = {}
    for c in range(chans):
        copies[0, c] = send(own.at[c], 0, c, right)
        copies[1, chans - 1 - c] = send(own.at[chans - 1 - c], 1, chans - 1 - c, left)
    copies[0, 0].wait_recv()
    copies[2, 0] = send(got.at[0, 0], 2, 0, right)
    copies[1, 1].wait_recv()
    copies[2, 1] = send(got.at[1, 1], 2, 1, left)
    operator = fit_operator(zern_ref[...], weight_ref[...], dft_ref[...])
    table = jnp.concatenate([operator[:, :CELLS], operator[:, CELLS:]], axis=0)
    high = table.astype(BF16)
    table_ref[: 2 * ZERN, :] = high
    table_ref[2 * ZERN :, :] = (table - high.astype(F32)).astype(BF16)
    for slot, c in ((0, 1), (1, 0), (2, 0), (2, 1)):
        copies[slot, c].wait_recv()
    for c in range(chans):
        total = own[c].astype(F32)
        for slot in range(3):
            total = total + got[slot, c].astype(F32)
        out_ref[c] = total
    for copy in copies.values():
        copy.wait_send()


def correlate_kernel(
    volt_ref, refs_ref, pos_ref, table_ref, out_ref, field, left_a, left_b,
    part, side, held, got, summed, last, side_send, side_recv, send_sem, recv_sem,
    last_send, last_recv,
):
    tm, q = lax.axis_index("tm"), lax.axis_index("chan")
    n_tm, n_q = lax.axis_size("tm"), lax.axis_size("chan")
    n_z = n_tm // 2
    x, z = tm // n_z, lax.rem(tm, n_z)
    other = 1 - x
    barrier = pltpu.get_barrier_semaphore()
    partner = {"tm": other * n_z + z}
    along = {d: {"tm": x * n_z + lax.rem(z + d, n_z)} for d in range(1, n_z)}
    across = {d: {"chan": lax.rem(q + d, n_q)} for d in range(1, n_q)}
    peers = [partner, *along.values(), *across.values()]
    for peer in peers:
        pl.semaphore_signal(barrier, inc=1, device_id=peer, device_id_type=MESH)
    chans, parts, stations, times = volt_ref.shape
    step = 512
    for t in range(0, times, step):
        cells = lax.broadcasted_iota(jnp.int32, (CELLS, step), 0)
        onehot = jnp.where(cells == pos_ref[:, t : t + step], 1.0, 0.0).astype(BF16)
        both = jnp.dot(table_ref[...], onehot, preferred_element_type=F32)
        field[:, t : t + step] = both[: 2 * ZERN] + both[2 * ZERN :]
    lane = lax.broadcasted_iota(jnp.int32, (stations, 2 * ZERN), 1)
    rows, width = 16, 256

    def build(left, c, r):
        for t in range(0, times, width):
            at = slice(t, t + width)
            re = jnp.broadcast_to(refs_ref[c, pl.ds(r, 1), at], (rows, width))
            im = jnp.broadcast_to(refs_ref[c, pl.ds(r + REFS, 1), at], (rows, width))
            for j in range(0, ZERN, rows):
                h = field[j : j + rows, at]
                g = field[ZERN + j : ZERN + j + rows, at]
                for base, value in ((j, re * h + im * g), (ZERN + j, re * g - im * h)):
                    high = value.astype(BF16)
                    left[base : base + rows, at] = high
                    low = (value - high.astype(F32)).astype(BF16)
                    left[2 * ZERN + base : 2 * ZERN + base + rows, at] = low

    def multiply(left, c, r):
        block = volt_ref[c].reshape(parts * stations, times)
        both = lax.dot_general(block, left[...], NT, preferred_element_type=F32)
        both = both[:, : 2 * ZERN] + both[:, 2 * ZERN :]
        real, imag = both[:stations], pltpu.roll(both[stations:], ZERN, 1)
        out = real + jnp.where(lane < ZERN, -imag, imag)
        part[c, pl.ds(r, stations, stride=REFS), :] = out

    def run(c, first, stop):
        def body(i, carry):
            r = 2 * i
            build(left_b, c, r + 1)
            multiply(left_a, c, r)
            follow = r + 2
            wrap = follow == REFS
            build(left_a, jnp.where(wrap, min(c + 1, chans - 1), c), jnp.where(wrap, 0, follow))
            multiply(left_b, c, r + 1)
            return carry

        lax.fori_loop(first, stop, body, 0)

    own = stations // (n_tm * n_q)
    chunk = own * REFS
    group = chunk * n_q
    order = sorted(range(n_z), key=lambda d: -min(d, n_z - d))

    def block(side_x, dz):
        start = (side_x * n_z + lax.rem(z + dz, n_z)) * group
        return pl.ds(pl.multiple_of(start, group), group)

    def send(src, dst, send, recv, peer):
        copy = pltpu.make_async_remote_copy(
            src_ref=src, dst_ref=dst, send_sem=send, recv_sem=recv,
            device_id=peer, device_id_type=MESH,
        )
        copy.start()
        return copy

    over, copies, final = {}, {}, {}

    def swap(c):
        for k, dz in enumerate(order):
            over[c, k] = send(
                part.at[c, block(other, dz)], side.at[c, k], side_send.at[c, k],
                side_recv.at[c, k], partner,
            )

    def forward(c, k):
        dz = order[k]
        over[c, k].wait_recv()
        held[c, k] = part[c, block(x, dz)] + side[c, k]
        if dz:
            copies[c, k] = send(
                held.at[c, k], got.at[c, k], send_sem.at[c, k], recv_sem.at[c, k], along[dz]
            )

    def reduce(c):
        total = held[c, n_z - 1]
        for k in range(n_z - 1):
            copies[c, k].wait_recv()
            total = total + got[c, k]
        summed[c] = total
        for d in range(1, n_q):
            aim = pl.multiple_of(lax.rem(q + d, n_q) * chunk, chunk)
            final[c, d] = send(
                summed.at[c, pl.ds(aim, chunk)], last.at[c, d - 1], last_send.at[c, d - 1],
                last_recv.at[c, d - 1], across[d],
            )

    def place(c, d, rows):
        origin = lax.rem(q - d + n_q, n_q)
        at = pl.ds(pl.multiple_of((origin * chans + c) * REFS, REFS), REFS)
        for s in range(own):
            out_ref[s, at] = rows[s * REFS : (s + 1) * REFS]

    build(left_a, 0, 0)
    run(0, 0, REFS // 2)
    pl.semaphore_wait(barrier, len(peers))
    swap(0)
    run(1, 0, REFS // 4)
    forward(0, 0)
    run(1, REFS // 4, REFS // 2)
    swap(1)
    for k in range(1, n_z):
        forward(0, k)
    for k in range(n_z - 2):
        forward(1, k)
    reduce(0)
    for k in range(n_z - 2, n_z):
        forward(1, k)
    reduce(1)
    for c in range(chans):
        place(c, 0, summed[c, pl.ds(pl.multiple_of(q * chunk, chunk), chunk)])
    for (c, d), copy in final.items():
        copy.wait_recv()
        place(c, d, last[c, d - 1])
    for copy in (*over.values(), *copies.values(), *final.values()):
        copy.wait_send()


def on_device(voltages, ref_index, positions, aperture_weight):
    chans, parts, stations, times = voltages.shape
    n_stat, n_tm, n_q = lax.axis_size("stat"), lax.axis_size("tm"), lax.axis_size("chan")
    scale = (n_tm * times / CELLS) ** (-0.5)
    zern = jnp.asarray(zernike_table())
    dft = jnp.asarray(dft_table(scale))
    vmem = pl.BlockSpec(memory_space=pltpu.VMEM)
    dma = pltpu.SemaphoreType.DMA
    refs, table = pl.pallas_call(
        exchange_kernel,
        out_shape=(
            jax.ShapeDtypeStruct((chans, 2 * REFS, times), F32),
            jax.ShapeDtypeStruct((4 * ZERN, CELLS), BF16),
        ),
        in_specs=[vmem, pl.BlockSpec(memory_space=pltpu.SMEM), vmem, vmem, vmem],
        out_specs=(vmem, vmem),
        scratch_shapes=[
            pltpu.VMEM((chans, 2 * REFS, times), BF16),
            pltpu.VMEM((n_stat - 1, chans, 2 * REFS, times), BF16),
            dma((n_stat - 1, chans)),
            dma((n_stat - 1, chans)),
        ],
        compiler_params=pltpu.CompilerParams(collective_id=0, has_side_effects=True),
        name="exchange",
    )(voltages, ref_index, zern, aperture_weight[None, :], dft)
    n_z = n_tm // 2
    own = stations // (n_tm * n_q)
    group = n_q * own * REFS
    wide = 2 * ZERN
    out = pl.pallas_call(
        correlate_kernel,
        out_shape=jax.ShapeDtypeStruct((own, n_q * chans * REFS, wide), F32),
        in_specs=[vmem] * 4,
        out_specs=vmem,
        scratch_shapes=[
            pltpu.VMEM((wide, times), F32),
            pltpu.VMEM((2 * wide, times), BF16),
            pltpu.VMEM((2 * wide, times), BF16),
            pltpu.VMEM((chans, stations * REFS, wide), F32),
            pltpu.VMEM((chans, n_z, group, wide), F32),
            pltpu.VMEM((chans, n_z, group, wide), F32),
            pltpu.VMEM((chans, n_z - 1, group, wide), F32),
            pltpu.VMEM((chans, group, wide), F32),
            pltpu.VMEM((chans, n_q - 1, own * REFS, wide), F32),
            dma((chans, n_z)),
            dma((chans, n_z)),
            dma((chans, n_z - 1)),
            dma((chans, n_z - 1)),
            dma((chans, n_q - 1)),
            dma((chans, n_q - 1)),
        ],
        compiler_params=pltpu.CompilerParams(collective_id=1, has_side_effects=True),
        name="correlate",
    )(voltages, refs, positions[None, :], table)
    return out.reshape(own, n_q * chans, REFS, 2 * ZERN)


def solution(mesh):
    in_specs = (P("chan", None, "stat", "tm"), P(), P("tm"), P())
    out_specs = P(("stat", "tm", "chan"), None, None, None)
    return jax.shard_map(
        on_device, mesh=mesh, in_specs=in_specs, out_specs=out_specs, check_vma=False
    )
```

time: 61.5 us -> 49.8 us (0.81)
  Pallas kernels: 58.4 us -> 48.1 us
  local copies, waits for them, and re-layouts: 2.81 us -> 1.47 us
    pallas_call x2 -> x1, Pallas kernels: 45.9 us -> 33.6 us  [on_device(): pl.pallas_call(correlate_kernel, out_shape=jax.ShapeDtypeStruct((own, n_q...]
    pallas_call x1, Pallas kernels: 12.5 us -> 14.6 us  [on_device(): pl.pallas_call(exchange_kernel, out_shape=(jax.ShapeDtypeStruct((chans, 2...]
    another operation x2 -> x0, local copies, waits for them, and re-layouts: 1.34 us -> none  [on_device(): index = jnp.tile(ref_index, 2)[:, None]]
where the time goes in v1:
time: 49.8 us; the launch traced here: 49.6 us
  Pallas kernels  48.1 us (97%)
  local copies, waits for them, and re-layouts  1.47 us (3%)
    pallas_call x1, Pallas kernels, on_device(): pl.pallas_call(correlate_kernel, out_shape=jax.ShapeDtypeStruct((own, n_q...  33.6 us
    pallas_call x1, Pallas kernels, on_device(): pl.pallas_call(exchange_kernel, out_shape=(jax.ShapeDtypeStruct((chans, 2...  14.6 us
    unnamed x1, local copies, waits for them, and re-layouts  1.47 us

profile of v1, /device:TPU:1, one launch (start us, length us, event | category | flops | bytes accessed | tf_op | source)
XLA Modules:
  0.0 49.6 jit_solution(9215304596145965681)
XLA Ops:
  0.0 14.6 %exchange.1 = (f32[2,16,2048]{2,1,0:T(8,128)}, bf16[256,256]{1,0:T(8,128)(2,1)}) custom-call(bf16[2,2,128,2048]{3,2,1,0:T(8,128)(2,1)} %volt_ref.3, s32[8]{0:T(128)} %index_ref.1, f32[64,256]{1,0:T(8,128)} %constant.4.clone.zern_ref, f32[1,256]{1,0:T(1,128)} %bitcast.5, f32[256,512]{1,0:T(8,128)} %constant.5.clone.dft_ref), custom_call_target="tpu_custom_call" | custom-call | tf_op jit(solution)/shard_map/exchange/pallas_call | solution.py:286
  14.6 33.6 %correlate.1 = f32[2,64,128]{2,1,0:T(8,128)} custom-call(bf16[2,2,128,2048]{3,2,1,0:T(8,128)(2,1)} %volt_ref.3, f32[2,16,2048]{2,1,0:T(8,128)} %get-tuple-element.7.refs_ref, s32[1,2048]{1,0:T(1,128)} %bitcast.4, bf16[256,256]{1,0:T(8,128)(2,1)} %get-tuple-element.8.table_ref), custom_call_target="tpu_custom_call" | custom-call | tf_op jit(solution)/shard_map/correlate/pallas_call | solution.py:307
  48.2 1.5 %copy.8 = f32[2,8,8,128]{3,2,1,0:T(8,128)} copy(f32[2,8,8,128]{3,2,1,0:T(8,128)} %bitcast.3) | data formatting | bytes 131072

commit v2 on v1

--- a/solution.py
+++ b/solution.py
@@ -61,7 +61,7 @@
     return (both * scale).astype(np.float32)
 
 
-def fit_operator(zern, weight, dft):
+def invert_gram(zern, weight):
     weighted = zern * weight
     gram = lax.dot_general(weighted, zern, NT, precision=HIGHEST, preferred_element_type=F32)
     rows = lax.broadcasted_iota(jnp.int32, (ZERN, ZERN), 0)
@@ -72,6 +72,10 @@
         pivot_row = both[k : k + 1, :] * (1.0 / both[k : k + 1, k : k + 1])
         reduced = both - both[:, k : k + 1] * pivot_row
         both = jnp.where(row_ids == k, pivot_row, reduced)
+    return weighted, both
+
+
+def fit_operator(weighted, both, dft):
     padded = jnp.concatenate([jnp.zeros_like(weighted), weighted], axis=0)
     solve = jnp.dot(both, padded, precision=HIGHEST, preferred_element_type=F32)
     return jnp.dot(solve, dft, precision=HIGHEST, preferred_element_type=F32)
@@ -79,7 +83,7 @@
 
 def exchange_kernel(
     volt_ref, index_ref, zern_ref, weight_ref, dft_ref, out_ref, table_ref,
-    own, got, send_sem, recv_sem,
+    own, got, inverse_ref, send_sem, recv_sem,
 ):
     n = lax.axis_size("stat")
     me = lax.axis_index("stat")
@@ -114,11 +118,13 @@
     for c in range(chans):
         copies[0, c] = send(own.at[c], 0, c, right)
         copies[1, chans - 1 - c] = send(own.at[chans - 1 - c], 1, chans - 1 - c, left)
+    weighted, inverse = invert_gram(zern_ref[...], weight_ref[...])
+    inverse_ref[...] = inverse
     copies[0, 0].wait_recv()
     copies[2, 0] = send(got.at[0, 0], 2, 0, right)
     copies[1, 1].wait_recv()
     copies[2, 1] = send(got.at[1, 1], 2, 1, left)
-    operator = fit_operator(zern_ref[...], weight_ref[...], dft_ref[...])
+    operator = fit_operator(weighted, inverse_ref[...], dft_ref[...])
     table = jnp.concatenate([operator[:, :CELLS], operator[:, CELLS:]], axis=0)
     high = table.astype(BF16)
     table_ref[: 2 * ZERN, :] = high
@@ -199,7 +205,13 @@
     own = stations // (n_tm * n_q)
     chunk = own * REFS
     group = chunk * n_q
-    order = sorted(range(n_z), key=lambda d: -min(d, n_z - d))
+    far = n_z // 2
+    order = [far]
+    for d in range(far - 1, 0, -1):
+        order += [d, n_z - d]
+    order.remove(far + 1)
+    order.insert(4, far + 1)
+    order.append(0)
 
     def block(side_x, dz):
         start = (side_x * n_z + lax.rem(z + dz, n_z)) * group
@@ -225,15 +237,20 @@
     def forward(c, k):
         dz = order[k]
         over[c, k].wait_recv()
-        held[c, k] = part[c, block(x, dz)] + side[c, k]
+        total = part[c, block(x, dz)] + side[c, k]
+        if dz == far + 1:
+            copies[c, 0].wait_recv()
+            total = total + got[c, 0]
+        held[c, k] = total
         if dz:
             copies[c, k] = send(
-                held.at[c, k], got.at[c, k], send_sem.at[c, k], recv_sem.at[c, k], along[dz]
+                held.at[c, k], got.at[c, k], send_sem.at[c, k], recv_sem.at[c, k],
+                along[n_z - 1 if dz == far else dz],
             )
 
     def reduce(c):
         total = held[c, n_z - 1]
-        for k in range(n_z - 1):
+        for k in range(1, n_z - 1):
             copies[c, k].wait_recv()
             total = total + got[c, k]
         summed[c] = total
@@ -294,6 +311,7 @@
         scratch_shapes=[
             pltpu.VMEM((chans, 2 * REFS, times), BF16),
             pltpu.VMEM((n_stat - 1, chans, 2 * REFS, times), BF16),
+            pltpu.VMEM((ZERN, 2 * ZERN), F32),
             dma((n_stat - 1, chans)),
             dma((n_stat - 1, chans)),
         ],

time: 49.8 us -> 50.7 us (1.018)
  Pallas kernels: 48.1 us -> 49 us
    pallas_call x1, Pallas kernels: 33.6 us -> 35 us  [on_device(): pl.pallas_call(correlate_kernel, out_shape=jax.ShapeDtypeStruct((own, n_q...]
    pallas_call x1, Pallas kernels: 14.6 us -> 14 us  [on_device(): pl.pallas_call(exchange_kernel, out_shape=(jax.ShapeDtypeStruct((chans, 2...]
where the time goes in v2:
time: 50.7 us; the launch traced here: 50.5 us
  Pallas kernels  49 us (97%)
  local copies, waits for them, and re-layouts  1.47 us (3%)
    pallas_call x1, Pallas kernels, on_device(): pl.pallas_call(correlate_kernel, out_shape=jax.ShapeDtypeStruct((own, n_q...  35 us
    pallas_call x1, Pallas kernels, on_device(): pl.pallas_call(exchange_kernel, out_shape=(jax.ShapeDtypeStruct((chans, 2...  14 us
    unnamed x1, local copies, waits for them, and re-layouts  1.47 us

profile of v2, /device:TPU:1, one launch (start us, length us, event | category | flops | bytes accessed | tf_op | source)
XLA Modules:
  0.0 50.5 jit_solution(804703628836501159)
XLA Ops:
  0.0 14.0 %exchange.1 = (f32[2,16,2048]{2,1,0:T(8,128)}, bf16[256,256]{1,0:T(8,128)(2,1)}) custom-call(bf16[2,2,128,2048]{3,2,1,0:T(8,128)(2,1)} %volt_ref.3, s32[8]{0:T(128)} %index_ref.1, f32[64,256]{1,0:T(8,128)} %constant.4.clone.zern_ref, f32[1,256]{1,0:T(1,128)} %bitcast.5, f32[256,512]{1,0:T(8,128)} %constant.5.clone.dft_ref), custom_call_target="tpu_custom_call" | custom-call | tf_op jit(solution)/shard_map/exchange/pallas_call | solution.py:303
  14.0 35.0 %correlate.1 = f32[2,64,128]{2,1,0:T(8,128)} custom-call(bf16[2,2,128,2048]{3,2,1,0:T(8,128)(2,1)} %volt_ref.3, f32[2,16,2048]{2,1,0:T(8,128)} %get-tuple-element.7.refs_ref, s32[1,2048]{1,0:T(1,128)} %bitcast.4, bf16[256,256]{1,0:T(8,128)(2,1)} %get-tuple-element.8.table_ref), custom_call_target="tpu_custom_call" | custom-call | tf_op jit(solution)/shard_map/correlate/pallas_call | solution.py:325
  49.0 1.5 %copy.8 = f32[2,8,8,128]{3,2,1,0:T(8,128)} copy(f32[2,8,8,128]{3,2,1,0:T(8,128)} %bitcast.3) | data formatting | bytes 131072

commit v3 on v1

--- a/solution.py
+++ b/solution.py
@@ -61,7 +61,7 @@
     return (both * scale).astype(np.float32)
 
 
-def fit_operator(zern, weight, dft):
+def invert_gram(zern, weight):
     weighted = zern * weight
     gram = lax.dot_general(weighted, zern, NT, precision=HIGHEST, preferred_element_type=F32)
     rows = lax.broadcasted_iota(jnp.int32, (ZERN, ZERN), 0)
@@ -72,14 +72,18 @@
         pivot_row = both[k : k + 1, :] * (1.0 / both[k : k + 1, k : k + 1])
         reduced = both - both[:, k : k + 1] * pivot_row
         both = jnp.where(row_ids == k, pivot_row, reduced)
+    return weighted, both
+
+
+def fit_operator(weighted, both, dft):
     padded = jnp.concatenate([jnp.zeros_like(weighted), weighted], axis=0)
     solve = jnp.dot(both, padded, precision=HIGHEST, preferred_element_type=F32)
     return jnp.dot(solve, dft, precision=HIGHEST, preferred_element_type=F32)
 
 
 def exchange_kernel(
-    volt_ref, index_ref, zern_ref, weight_ref, dft_ref, out_ref, table_ref,
-    own, got, send_sem, recv_sem,
+    volt_hbm, index_ref, zern_ref, weight_ref, dft_hbm, out_ref, table_ref,
+    volt_ref, dft_ref, own, got, inverse_ref, load_sem, send_sem, recv_sem,
 ):
     n = lax.axis_size("stat")
     me = lax.axis_index("stat")
@@ -88,6 +92,13 @@
     barrier = pltpu.get_barrier_semaphore()
     for peer in (right, left):
         pl.semaphore_signal(barrier, inc=1, device_id={"stat": peer}, device_id_type=MESH)
+    loads = [
+        pltpu.make_async_copy(volt_hbm.at[c], volt_ref.at[c], load_sem.at[c])
+        for c in range(chans)
+    ]
+    loads.append(pltpu.make_async_copy(dft_hbm, dft_ref, load_sem.at[chans]))
+    for load in loads:
+        load.start()
     cols = lax.broadcasted_iota(jnp.int32, (2 * REFS, parts * stations), 1)
     rows = lax.broadcasted_iota(jnp.int32, (2 * REFS, parts * stations), 0)
     wanted = jnp.zeros_like(rows)
@@ -98,6 +109,7 @@
     target = jnp.where(inside, wanted, -parts * stations) + (rows // REFS) * stations
     select = jnp.where(cols == target, 1.0, 0.0).astype(BF16)
     for c in range(chans):
+        loads[c].wait()
         block = volt_ref[c].reshape(parts * stations, times)
         own[c] = jnp.dot(select, block, preferred_element_type=F32).astype(BF16)
     pl.semaphore_wait(barrier, 2)
@@ -114,11 +126,14 @@
     for c in range(chans):
         copies[0, c] = send(own.at[c], 0, c, right)
         copies[1, chans - 1 - c] = send(own.at[chans - 1 - c], 1, chans - 1 - c, left)
+    weighted, inverse = invert_gram(zern_ref[...], weight_ref[...])
+    inverse_ref[...] = inverse
     copies[0, 0].wait_recv()
     copies[2, 0] = send(got.at[0, 0], 2, 0, right)
     copies[1, 1].wait_recv()
     copies[2, 1] = send(got.at[1, 1], 2, 1, left)
-    operator = fit_operator(zern_ref[...], weight_ref[...], dft_ref[...])
+    loads[chans].wait()
+    operator = fit_operator(weighted, inverse_ref[...], dft_ref[...])
     table = jnp.concatenate([operator[:, :CELLS], operator[:, CELLS:]], axis=0)
     high = table.astype(BF16)
     table_ref[: 2 * ZERN, :] = high
@@ -135,9 +150,9 @@
 
 
 def correlate_kernel(
-    volt_ref, refs_ref, pos_ref, table_ref, out_ref, field, left_a, left_b,
+    volt_hbm, refs_ref, pos_ref, table_ref, out_ref, volt_ref, field, left_a, left_b,
     part, side, held, got, summed, last, side_send, side_recv, send_sem, recv_sem,
-    last_send, last_recv,
+    last_send, last_recv, load_sem,
 ):
     tm, q = lax.axis_index("tm"), lax.axis_index("chan")
     n_tm, n_q = lax.axis_size("tm"), lax.axis_size("chan")
@@ -152,6 +167,12 @@
     for peer in peers:
         pl.semaphore_signal(barrier, inc=1, device_id=peer, device_id_type=MESH)
     chans, parts, stations, times = volt_ref.shape
+    loads = [
+        pltpu.make_async_copy(volt_hbm.at[c], volt_ref.at[c], load_sem.at[c])
+        for c in range(chans)
+    ]
+    for load in loads:
+        load.start()
     step = 512
     for t in range(0, times, step):
         cells = lax.broadcasted_iota(jnp.int32, (CELLS, step), 0)
@@ -251,6 +272,8 @@
             out_ref[s, at] = rows[s * REFS : (s + 1) * REFS]
 
     build(left_a, 0, 0)
+    for load in loads:
+        load.wait()
     run(0, 0, REFS // 2)
     pl.semaphore_wait(barrier, len(peers))
     swap(0)
@@ -282,6 +305,7 @@
     zern = jnp.asarray(zernike_table())
     dft = jnp.asarray(dft_table(scale))
     vmem = pl.BlockSpec(memory_space=pltpu.VMEM)
+    hbm = pl.BlockSpec(memory_space=pl.ANY)
     dma = pltpu.SemaphoreType.DMA
     refs, table = pl.pallas_call(
         exchange_kernel,
@@ -289,11 +313,15 @@
             jax.ShapeDtypeStruct((chans, 2 * REFS, times), F32),
             jax.ShapeDtypeStruct((4 * ZERN, CELLS), BF16),
         ),
-        in_specs=[vmem, pl.BlockSpec(memory_space=pltpu.SMEM), vmem, vmem, vmem],
+        in_specs=[hbm, pl.BlockSpec(memory_space=pltpu.SMEM), vmem, vmem, hbm],
         out_specs=(vmem, vmem),
         scratch_shapes=[
+            pltpu.VMEM(voltages.shape, BF16),
+            pltpu.VMEM(dft.shape, F32),
             pltpu.VMEM((chans, 2 * REFS, times), BF16),
             pltpu.VMEM((n_stat - 1, chans, 2 * REFS, times), BF16),
+            pltpu.VMEM((ZERN, 2 * ZERN), F32),
+            dma((chans + 1,)),
             dma((n_stat - 1, chans)),
             dma((n_stat - 1, chans)),
         ],
@@ -307,9 +335,10 @@
     out = pl.pallas_call(
         correlate_kernel,
         out_shape=jax.ShapeDtypeStruct((own, n_q * chans * REFS, wide), F32),
-        in_specs=[vmem] * 4,
+        in_specs=[hbm, vmem, vmem, vmem],
         out_specs=vmem,
         scratch_shapes=[
+            pltpu.VMEM(voltages.shape, BF16),
             pltpu.VMEM((wide, times), F32),
             pltpu.VMEM((2 * wide, times), BF16),
             pltpu.VMEM((2 * wide, times), BF16),
@@ -325,6 +354,7 @@
             dma((chans, n_z - 1)),
             dma((chans, n_q - 1)),
             dma((chans, n_q - 1)),
+            dma((chans,)),
         ],
         compiler_params=pltpu.CompilerParams(collective_id=1, has_side_effects=True),
         name="correlate",

time: 49.8 us -> 50 us (level)
  no operation moved by 1% of the time
where the time goes in v3:
time: 50 us; the launch traced here: 49.8 us
  Pallas kernels  48.3 us (97%)
  local copies, waits for them, and re-layouts  1.47 us (3%)
    pallas_call x1, Pallas kernels, on_device(): pl.pallas_call(correlate_kernel, out_shape=jax.ShapeDtypeStruct((own, n_q...  33.8 us
    pallas_call x1, Pallas kernels, on_device(): pl.pallas_call(exchange_kernel, out_shape=(jax.ShapeDtypeStruct((chans, 2...  14.5 us
    unnamed x1, local copies, waits for them, and re-layouts  1.47 us

profile of v3, /device:TPU:1, one launch (start us, length us, event | category | flops | bytes accessed | tf_op | source)
XLA Modules:
  0.0 49.8 jit_solution(3930861935193675942)
XLA Ops:
  0.0 14.5 %exchange.1 = (f32[2,16,2048]{2,1,0:T(8,128)}, bf16[256,256]{1,0:T(8,128)(2,1)}) custom-call(bf16[2,2,128,2048]{3,2,1,0:T(8,128)(2,1)} %volt_hbm.3, s32[8]{0:T(128)} %index_ref.1, f32[64,256]{1,0:T(8,128)} %constant.4.clone.zern_ref, f32[1,256]{1,0:T(1,128)} %bitcast.5, f32[256,512]{1,0:T(8,128)} %constant.5.clone.dft_hbm), custom_call_target="tpu_custom_call" | custom-call | tf_op jit(solution)/shard_map/exchange/pallas_call | solution.py:310
  14.5 33.8 %correlate.1 = f32[2,64,128]{2,1,0:T(8,128)} custom-call(bf16[2,2,128,2048]{3,2,1,0:T(8,128)(2,1)} %volt_hbm.3, f32[2,16,2048]{2,1,0:T(8,128)} %get-tuple-element.7.refs_ref, s32[1,2048]{1,0:T(1,128)} %bitcast.4, bf16[256,256]{1,0:T(8,128)(2,1)} %get-tuple-element.8.table_ref), custom_call_target="tpu_custom_call" | custom-call | tf_op jit(solution)/shard_map/correlate/pallas_call | solution.py:335
  48.3 1.5 %copy.8 = f32[2,8,8,128]{3,2,1,0:T(8,128)} copy(f32[2,8,8,128]{3,2,1,0:T(8,128)} %bitcast.3) | data formatting | bytes 131072

commit v4 on v3

--- a/solution.py
+++ b/solution.py
@@ -152,7 +152,7 @@
 def correlate_kernel(
     volt_hbm, refs_ref, pos_ref, table_ref, out_ref, volt_ref, field, left_a, left_b,
     part, side, held, got, summed, last, side_send, side_recv, send_sem, recv_sem,
-    last_send, last_recv, load_sem,
+    last_send, last_recv, load_sem, cross, joined, cross_send, cross_recv,
 ):
     tm, q = lax.axis_index("tm"), lax.axis_index("chan")
     n_tm, n_q = lax.axis_size("tm"), lax.axis_size("chan")
@@ -234,14 +234,37 @@
         copy.start()
         return copy
 
-    over, copies, final = {}, {}, {}
+    near = ((1, n_z - 1, 2, n_z - 2), (1, n_z - 1))
+    rest = [[k for k, d in enumerate(order) if d and d not in near[c]] for c in range(chans)]
+    home = n_z - 1
+    over, copies, final, crossed = {}, {}, {}, {}
 
     def swap(c):
-        for k, dz in enumerate(order):
+        for k in rest[c]:
             over[c, k] = send(
-                part.at[c, block(other, dz)], side.at[c, k], side_send.at[c, k],
+                part.at[c, block(other, order[k])], side.at[c, k], side_send.at[c, k],
                 side_recv.at[c, k], partner,
             )
+        for i, d in enumerate(near[c]):
+            k = order.index(d)
+            crossed[c, i] = send(
+                part.at[c, block(other, d)], cross.at[c, i], cross_send.at[c, i],
+                cross_recv.at[c, i], along[d],
+            )
+            copies[c, k] = send(
+                part.at[c, block(x, d)], got.at[c, k], send_sem.at[c, k], recv_sem.at[c, k],
+                along[d],
+            )
+
+    def swap_last(c):
+        total = part[c, block(other, 0)]
+        for i in range(len(near[c])):
+            crossed[c, i].wait_recv()
+            total = total + cross[c, i]
+        joined[c] = total
+        over[c, home] = send(
+            joined.at[c], side.at[c, home], side_send.at[c, home], side_recv.at[c, home], partner
+        )
 
     def forward(c, k):
         dz = order[k]
@@ -281,20 +304,24 @@
     forward(0, 0)
     run(1, REFS // 4, REFS // 2)
     swap(1)
-    for k in range(1, n_z):
+    swap_last(0)
+    for k in rest[0][1:]:
         forward(0, k)
-    for k in range(n_z - 2):
+    for k in rest[1][:3]:
         forward(1, k)
+    swap_last(1)
+    for k in rest[1][3:]:
+        forward(1, k)
+    forward(0, home)
     reduce(0)
-    for k in range(n_z - 2, n_z):
-        forward(1, k)
+    forward(1, home)
     reduce(1)
     for c in range(chans):
         place(c, 0, summed[c, pl.ds(pl.multiple_of(q * chunk, chunk), chunk)])
     for (c, d), copy in final.items():
         copy.wait_recv()
         place(c, d, last[c, d - 1])
-    for copy in (*over.values(), *copies.values(), *final.values()):
+    for copy in (*over.values(), *copies.values(), *crossed.values(), *final.values()):
         copy.wait_send()
 
 
@@ -355,6 +382,10 @@
             dma((chans, n_q - 1)),
             dma((chans, n_q - 1)),
             dma((chans,)),
+            pltpu.VMEM((chans, 4, group, wide), F32),
+            pltpu.VMEM((chans, group, wide), F32),
+            dma((chans, 4)),
+            dma((chans, 4)),
         ],
         compiler_params=pltpu.CompilerParams(collective_id=1, has_side_effects=True),
         name="correlate",

time: 50 us -> 49.5 us (0.990)
  Pallas kernels: 48.3 us -> 47.8 us
    pallas_call x1, Pallas kernels: 33.8 us -> 33.3 us  [on_device(): pl.pallas_call(correlate_kernel, out_shape=jax.ShapeDtypeStruct((own, n_q...]
where the time goes in v4:
time: 49.5 us; the launch traced here: 49.3 us
  Pallas kernels  47.8 us (97%)
  local copies, waits for them, and re-layouts  1.47 us (3%)
    pallas_call x1, Pallas kernels, on_device(): pl.pallas_call(correlate_kernel, out_shape=jax.ShapeDtypeStruct((own, n_q...  33.3 us
    pallas_call x1, Pallas kernels, on_device(): pl.pallas_call(exchange_kernel, out_shape=(jax.ShapeDtypeStruct((chans, 2...  14.5 us
    unnamed x1, local copies, waits for them, and re-layouts  1.47 us

profile of v4, /device:TPU:1, one launch (start us, length us, event | category | flops | bytes accessed | tf_op | source)
XLA Modules:
  0.0 49.3 jit_solution(621119239815582392)
XLA Ops:
  0.0 14.5 %exchange.1 = (f32[2,16,2048]{2,1,0:T(8,128)}, bf16[256,256]{1,0:T(8,128)(2,1)}) custom-call(bf16[2,2,128,2048]{3,2,1,0:T(8,128)(2,1)} %volt_hbm.3, s32[8]{0:T(128)} %index_ref.1, f32[64,256]{1,0:T(8,128)} %constant.4.clone.zern_ref, f32[1,256]{1,0:T(1,128)} %bitcast.5, f32[256,512]{1,0:T(8,128)} %constant.5.clone.dft_hbm), custom_call_target="tpu_custom_call" | custom-call | tf_op jit(solution)/shard_map/exchange/pallas_call | solution.py:337
  14.5 33.3 %correlate.1 = f32[2,64,128]{2,1,0:T(8,128)} custom-call(bf16[2,2,128,2048]{3,2,1,0:T(8,128)(2,1)} %volt_hbm.3, f32[2,16,2048]{2,1,0:T(8,128)} %get-tuple-element.7.refs_ref, s32[1,2048]{1,0:T(1,128)} %bitcast.4, bf16[256,256]{1,0:T(8,128)(2,1)} %get-tuple-element.8.table_ref), custom_call_target="tpu_custom_call" | custom-call | tf_op jit(solution)/shard_map/correlate/pallas_call | solution.py:362
  47.8 1.5 %copy.8 = f32[2,8,8,128]{3,2,1,0:T(8,128)} copy(f32[2,8,8,128]{3,2,1,0:T(8,128)} %bitcast.3) | data formatting | bytes 131072

commit v5 on v4

--- a/solution.py
+++ b/solution.py
@@ -220,7 +220,8 @@
     own = stations // (n_tm * n_q)
     chunk = own * REFS
     group = chunk * n_q
-    order = sorted(range(n_z), key=lambda d: -min(d, n_z - d))
+    far = n_z // 2
+    order = [far, far - 1, 2, far + 1, n_z - 2, 1, n_z - 1, 0]
 
     def block(side_x, dz):
         start = (side_x * n_z + lax.rem(z + dz, n_z)) * group
@@ -269,15 +270,20 @@
     def forward(c, k):
         dz = order[k]
         over[c, k].wait_recv()
-        held[c, k] = part[c, block(x, dz)] + side[c, k]
+        total = part[c, block(x, dz)] + side[c, k]
+        if dz == far + 1:
+            copies[c, 0].wait_recv()
+            total = total + got[c, 0]
+        held[c, k] = total
         if dz:
             copies[c, k] = send(
-                held.at[c, k], got.at[c, k], send_sem.at[c, k], recv_sem.at[c, k], along[dz]
+                held.at[c, k], got.at[c, k], send_sem.at[c, k], recv_sem.at[c, k],
+                along[n_z - 1 if dz == far else dz],
             )
 
     def reduce(c):
         total = held[c, n_z - 1]
-        for k in range(n_z - 1):
+        for k in range(1, n_z - 1):
             copies[c, k].wait_recv()
             total = total + got[c, k]
         summed[c] = total

time: 49.5 us -> 50.2 us (1.014)
  Pallas kernels: 47.8 us -> 48.5 us
    pallas_call x1, Pallas kernels: 33.3 us -> 34 us  [on_device(): pl.pallas_call(correlate_kernel, out_shape=jax.ShapeDtypeStruct((own, n_q...]
where the time goes in v5:
time: 50.2 us; the launch traced here: 50 us
  Pallas kernels  48.5 us (97%)
  local copies, waits for them, and re-layouts  1.47 us (3%)
    pallas_call x1, Pallas kernels, on_device(): pl.pallas_call(correlate_kernel, out_shape=jax.ShapeDtypeStruct((own, n_q...  34 us
    pallas_call x1, Pallas kernels, on_device(): pl.pallas_call(exchange_kernel, out_shape=(jax.ShapeDtypeStruct((chans, 2...  14.5 us
    unnamed x1, local copies, waits for them, and re-layouts  1.47 us

profile of v5, /device:TPU:1, one launch (start us, length us, event | category | flops | bytes accessed | tf_op | source)
XLA Modules:
  0.0 50.0 jit_solution(14232522845587343392)
XLA Ops:
  0.0 14.5 %exchange.1 = (f32[2,16,2048]{2,1,0:T(8,128)}, bf16[256,256]{1,0:T(8,128)(2,1)}) custom-call(bf16[2,2,128,2048]{3,2,1,0:T(8,128)(2,1)} %volt_hbm.3, s32[8]{0:T(128)} %index_ref.1, f32[64,256]{1,0:T(8,128)} %constant.4.clone.zern_ref, f32[1,256]{1,0:T(1,128)} %bitcast.5, f32[256,512]{1,0:T(8,128)} %constant.5.clone.dft_hbm), custom_call_target="tpu_custom_call" | custom-call | tf_op jit(solution)/shard_map/exchange/pallas_call | solution.py:343
  14.5 34.0 %correlate.1 = f32[2,64,128]{2,1,0:T(8,128)} custom-call(bf16[2,2,128,2048]{3,2,1,0:T(8,128)(2,1)} %volt_hbm.3, f32[2,16,2048]{2,1,0:T(8,128)} %get-tuple-element.7.refs_ref, s32[1,2048]{1,0:T(1,128)} %bitcast.4, bf16[256,256]{1,0:T(8,128)(2,1)} %get-tuple-element.8.table_ref), custom_call_target="tpu_custom_call" | custom-call | tf_op jit(solution)/shard_map/correlate/pallas_call | solution.py:368
  48.5 1.5 %copy.8 = f32[2,8,8,128]{3,2,1,0:T(8,128)} copy(f32[2,8,8,128]{3,2,1,0:T(8,128)} %bitcast.3) | data formatting | bytes 131072

commit v6 on v4

--- a/solution.py
+++ b/solution.py
@@ -302,10 +302,12 @@
     swap(0)
     run(1, 0, REFS // 4)
     forward(0, 0)
-    run(1, REFS // 4, REFS // 2)
+    run(1, REFS // 4, REFS // 4 + 1)
+    forward(0, rest[0][1])
+    run(1, REFS // 4 + 1, REFS // 2)
     swap(1)
     swap_last(0)
-    for k in rest[0][1:]:
+    for k in rest[0][2:]:
         forward(0, k)
     for k in rest[1][:3]:
         forward(1, k)

time: 49.5 us -> 49.6 us (level)
  no operation moved by 1% of the time
where the time goes in v6:
time: 49.6 us; the launch traced here: 49.4 us
  Pallas kernels  47.9 us (97%)
  local copies, waits for them, and re-layouts  1.47 us (3%)
    pallas_call x1, Pallas kernels, on_device(): pl.pallas_call(correlate_kernel, out_shape=jax.ShapeDtypeStruct((own, n_q...  33.4 us
    pallas_call x1, Pallas kernels, on_device(): pl.pallas_call(exchange_kernel, out_shape=(jax.ShapeDtypeStruct((chans, 2...  14.5 us
    unnamed x1, local copies, waits for them, and re-layouts  1.47 us

profile of v6, /device:TPU:1, one launch (start us, length us, event | category | flops | bytes accessed | tf_op | source)
XLA Modules:
  0.0 49.4 jit_solution(7509343698216581564)
XLA Ops:
  0.0 14.5 %exchange.1 = (f32[2,16,2048]{2,1,0:T(8,128)}, bf16[256,256]{1,0:T(8,128)(2,1)}) custom-call(bf16[2,2,128,2048]{3,2,1,0:T(8,128)(2,1)} %volt_hbm.3, s32[8]{0:T(128)} %index_ref.1, f32[64,256]{1,0:T(8,128)} %constant.4.clone.zern_ref, f32[1,256]{1,0:T(1,128)} %bitcast.5, f32[256,512]{1,0:T(8,128)} %constant.5.clone.dft_hbm), custom_call_target="tpu_custom_call" | custom-call | tf_op jit(solution)/shard_map/exchange/pallas_call | solution.py:339
  14.5 33.4 %correlate.1 = f32[2,64,128]{2,1,0:T(8,128)} custom-call(bf16[2,2,128,2048]{3,2,1,0:T(8,128)(2,1)} %volt_hbm.3, f32[2,16,2048]{2,1,0:T(8,128)} %get-tuple-element.7.refs_ref, s32[1,2048]{1,0:T(1,128)} %bitcast.4, bf16[256,256]{1,0:T(8,128)(2,1)} %get-tuple-element.8.table_ref), custom_call_target="tpu_custom_call" | custom-call | tf_op jit(solution)/shard_map/correlate/pallas_call | solution.py:364
  47.9 1.5 %copy.8 = f32[2,8,8,128]{3,2,1,0:T(8,128)} copy(f32[2,8,8,128]{3,2,1,0:T(8,128)} %bitcast.3) | data formatting | bytes 131072
